TPU v7x, 32 devices: a whole 2x2x4 slice. The times are simulated.
32 devices in a mesh: outer: 4 (over x, core), inner: 8 (over z, y).
Axes of the slice: x: 2, y: 2, z: 4, core: 2. Of those that a mesh axis runs over, the one named last changes fastest.
Arguments:
- vertex: float32 [131072, 128], P(('outer', 'inner')), may hold values from -1.75 to 1.75
- context: float32 [65536, 128], P(('outer', 'inner')), may hold values from -1.75 to 1.75
- tile_count: int32 [128], P(('outer', 'inner')), may hold values from 1 to 8, as said below
- tile_vert: int32 [128, 8], P(('outer', 'inner')), may hold values from 0 to 15
- tile_context: int32 [128, 8], P(('outer', 'inner')), may hold values from 0 to 7
- positives: int32 [128, 8, 256], P(('outer', 'inner')), may hold values from 0 to 255
- negatives: int32 [128, 8, 4, 256], P(('outer', 'inner')), may hold values from 0 to 255
Outputs:
- vertex_out: float32 [131072, 128], P(('outer', 'inner'))
- context_out: float32 [65536, 128], P(('outer', 'inner'))
Inputs may be any that keep to these rules, and one draw needn't show every extreme that they name: `tile_count`: every entry is at least 1, and in every tour step some device has all 8 slots live.
All inputs are finite; a program needn't handle non-finite values.
Results may differ from a plain program's by a relative error of at most 0.0003.
Values sent between devices are 32-bit elements; how exact they have to be, the bound alone decides.
A program may use at most 64 MiB of HBM per device.

v0:
```python
import functools

import jax
import jax.numpy as jnp
from jax import lax
from jax.experimental import pallas as pl
from jax.experimental.pallas import tpu as pltpu
from jax.sharding import PartitionSpec as P

TILE = 256

learn_rate = 0.5

MESH = pl.DeviceIdType.MESH


def halves(x):
    high = x.astype(jnp.bfloat16)
    low = (x - high.astype(jnp.float32)).astype(jnp.bfloat16)
    return high, low


def dot(a, b, dims):
    return lax.dot_general(a, b, (dims, ((), ())), preferred_element_type=jnp.float32)


class Fields:
    def __init__(self, tiles, slots, ctiles):
        start = 0
        for name, size in (
            ("place", tiles), ("order", tiles), ("last", tiles), ("spot", slots), ("prev", slots),
            ("lastspot", slots), ("vert", slots), ("context", slots), ("prevc", slots),
            ("lastc", ctiles), ("count", 1),
        ):
            setattr(self, name, start)
            start += size
        self.width = -(-start // 128) * 128


def tables(tile_count, tile_vert, tile_context, tiles, ctiles):
    steps, slots = tile_vert.shape
    i32 = jnp.int32
    ks = jnp.arange(tiles, dtype=i32)
    cs = jnp.arange(ctiles, dtype=i32)
    ts = jnp.arange(slots, dtype=i32)
    is_tile = tile_vert[:, :, None] == ks
    marked = jnp.any(is_tile, 1).astype(i32)
    before = jnp.sum(jnp.where(ks[None, :, None] > ks[None, None, :], marked[:, None, :], 0), -1)
    total = jnp.sum(marked, -1, keepdims=True)
    place = jnp.where(marked == 1, before, total + ks - before)
    order = jnp.sum(jnp.where(place[:, None, :] == ks[None, :, None], ks, 0), -1)
    last = jnp.max(jnp.where(is_tile, ts[None, :, None], -1), 1)
    spot = jnp.sum(jnp.where(is_tile, place[:, None, :], 0), -1)
    earlier = ts[None, :, None] > ts[None, None, :]
    prev = jnp.max(jnp.where(earlier & (tile_vert[:, :, None] == tile_vert[:, None, :]), ts, -1), -1)
    lastspot = jnp.max(jnp.where(spot[:, None, :] == ts[None, :, None], ts, -1), -1)
    prevc = jnp.max(jnp.where(earlier & (tile_context[:, :, None] == tile_context[:, None, :]), ts, -1), -1)
    lastc = jnp.max(jnp.where(tile_context[:, None, :] == cs[None, :, None], ts, -1), -1)
    rows = jnp.concatenate(
        [place, order, last, spot, prev, lastspot, tile_vert, tile_context, prevc, lastc, tile_count[:, None]], 1
    )
    width = Fields(tiles, slots, ctiles).width
    return jnp.pad(rows, ((0, -steps % 8), (0, width - rows.shape[1])))


def kernel(
    sizes, meta, meta_s, vertex, context, positives, negatives, v_out, c_out,
    pool0, pool1, pool2, pool3, cpool0, cpool1, cpool2, cpool3,
    near0, far0, near1, near2, far2, near3, csend0, csend2, last, out,
    lists_v, lists, pos_home, neg_home, pos_role, neg_role, send, recv, local,
):
    tiles, slots, ctiles = sizes
    f = Fields(tiles, slots, ctiles)
    outer, inner = lax.axis_size("outer"), lax.axis_size("inner")
    o, i = lax.axis_index("outer"), lax.axis_index("inner")

    def swapped(o, i):
        return 2 * (o // 2) + i % 2, 2 * (i // 2) + o % 2

    def at(o, i):
        return (o + outer) % outer, (i + inner) % inner

    ro, ri = swapped(o, i)
    stays = o % 2 == i % 2

    def remote(source, target, k, device):
        return pltpu.make_async_remote_copy(
            src_ref=source, dst_ref=target, send_sem=send.at[k], recv_sem=recv.at[k],
            device_id=device, device_id_type=MESH,
        )

    here = [
        pltpu.make_async_copy(vertex, pool0.at[pl.ds(0, tiles)], local.at[0]),
        pltpu.make_async_copy(context, cpool0.at[pl.ds(0, ctiles)], local.at[1]),
        pltpu.make_async_copy(positives.at[pl.ds(0, 1)], pos_home.at[pl.ds(0, 1)], local.at[2]),
        pltpu.make_async_copy(negatives.at[pl.ds(0, 1)], neg_home.at[pl.ds(0, 1)], local.at[3]),
        pltpu.make_async_copy(positives.at[pl.ds(3, 1)], pos_home.at[pl.ds(1, 1)], local.at[4]),
        pltpu.make_async_copy(negatives.at[pl.ds(3, 1)], neg_home.at[pl.ds(1, 1)], local.at[5]),
    ]
    for copy in here:
        copy.start()

    sends = [
        remote(meta, lists_v.at[1], 1, at(o, i - 1)),
        remote(meta, lists_v.at[2], 2, swapped(*at(o, i + 1))),
        remote(meta, lists_v.at[3], 3, swapped(*at(o, i - 1))),
        remote(meta, lists_v.at[4], 4, at(o + 1, i)),
    ]
    for copy in sends:
        copy.start()
    role_copies = [
        remote(meta, lists_v.at[0], 0, (ro, ri)),
        remote(positives.at[pl.ds(1, 2)], pos_role, 5, (ro, ri)),
        remote(negatives.at[pl.ds(1, 2)], neg_role, 6, (ro, ri)),
    ]
    own_copies = [
        pltpu.make_async_copy(meta, lists_v.at[0], local.at[6]),
        pltpu.make_async_copy(positives.at[pl.ds(1, 2)], pos_role, local.at[7]),
        pltpu.make_async_copy(negatives.at[pl.ds(1, 2)], neg_role, local.at[8]),
    ]

    @pl.when(stays)
    def _():
        for copy in own_copies:
            copy.start()

    @pl.when(jnp.logical_not(stays))
    def _():
        for copy in role_copies:
            copy.start()

    rows = lax.broadcasted_iota(jnp.int32, (TILE, TILE), 0)
    group = 2 if slots % 2 == 0 else 1
    width = pool0.shape[-1]

    def train(count, vert_at, prev_at, context_at, prevc_at, step, pos, neg, pool, held, cpool):
        def slot_group(g, carry):
            work = []
            for j in range(group):
                t = g * group + j
                live = (t < count).astype(jnp.float32)
                work.append((t, vert_at(t), context_at(t), live))
            anchors = [halves(pool[w[1]]) for w in work]
            partners = [halves(cpool[w[2]]) for w in work]
            gradients = []
            for (t, _, _, live), (a_high, a_low), (p_high, p_low) in zip(work, anchors, partners):
                both = jnp.concatenate([a_high, a_low], 1)
                twice = jnp.concatenate([p_high, p_high], 1)
                scores = dot(twice, both, ((1,), (1,))) + dot(p_low, a_high, ((1,), (1,)))
                half = -0.5 * learn_rate * live
                change = half * jnp.tanh(0.5 * scores) + half
                gradient = jnp.where(pos[step, pl.ds(t, 1)] == rows, change + learn_rate * live, 0.0)
                for k in range(neg.shape[2]):
                    gradient += jnp.where(neg[step, t, pl.ds(k, 1)] == rows, change, 0.0)
                gradients.append(halves(gradient))
            for (t, at_v, at_c, _), (a_high, a_low), (p_high, p_low), (g_high, g_low) in zip(
                work, anchors, partners, gradients
            ):
                wide = dot(g_high, jnp.concatenate([p_high, p_low], 1), ((0,), (0,)))
                prev = prev_at(t)
                base = pool[jnp.where(prev < 0, at_v, held + prev)]
                pool[held + t] = base + (wide[:, :width] + wide[:, width:] + dot(g_low, p_high, ((0,), (0,))))
                wide = dot(g_high, jnp.concatenate([a_high, a_low], 1), ((1,), (0,)))
                prev = prevc_at(t)
                base = cpool[jnp.where(prev < 0, at_c, ctiles + prev)]
                cpool[ctiles + t] = base + (wide[:, :width] + wide[:, width:] + dot(g_low, a_high, ((1,), (0,))))
            return carry

        lax.fori_loop(0, slots // group, slot_group, 0)

    def pack(source, targets, index):
        p = 0
        for target, size in targets:
            for k in range(size):
                target[k] = source[index(p)]
                p += 1

    def context_index(row):
        def index(k):
            slot = row(f.lastc + k)
            return jnp.where(slot < 0, k, ctiles + slot)
        return index

    def mine(s):
        return lambda k: meta_s[s, k]

    def other(which, s):
        return lambda k: lists[which, s, k]

    for copy in here[:4]:
        copy.wait()
    m = mine(0)
    train(
        m(f.count), lambda t: m(f.vert + t), lambda t: m(f.prev + t), lambda t: m(f.context + t),
        lambda t: m(f.prevc + t), 0, pos_home, neg_home, pool0, tiles, cpool0,
    )
    for copy in sends:
        copy.wait()

    @pl.when(stays)
    def _():
        for copy in own_copies:
            copy.wait()

    @pl.when(jnp.logical_not(stays))
    def _():
        for copy in role_copies:
            copy.wait()

    to_smem = pltpu.make_async_copy(lists_v, lists, local.at[9])
    to_smem.start()
    to_smem.wait()

    after = other(1, 1)

    def index0(p):
        tile = after(f.order + p)
        slot = m(f.last + tile)
        return jnp.where(slot < 0, tile, tiles + slot)

    pack(pool0, ((near0, slots),), index0)
    send_near0 = remote(near0, pool1.at[pl.ds(0, slots)], 7, swapped(*at(o, i + 1)))
    send_near0.start()
    pack(cpool0, ((csend0, ctiles),), context_index(m))
    send_c0 = remote(csend0, cpool1.at[pl.ds(0, ctiles)], 8, (ro, ri))
    keep_c0 = pltpu.make_async_copy(csend0, cpool1.at[pl.ds(0, ctiles)], local.at[10])

    @pl.when(stays)
    def _():
        keep_c0.start()

    @pl.when(jnp.logical_not(stays))
    def _():
        send_c0.start()

    pack(pool0, ((far0, tiles - slots),), lambda p: index0(slots + p))
    send_far0 = remote(far0, pool2.at[pl.ds(slots, tiles - slots)], 9, swapped(*at(o, i + 2)))
    send_far0.start()

    send_near0.wait()

    @pl.when(stays)
    def _():
        keep_c0.wait()

    @pl.when(jnp.logical_not(stays))
    def _():
        send_c0.wait()

    r = other(0, 1)
    train(
        r(f.count), lambda t: r(f.spot + t), lambda t: r(f.prev + t), lambda t: r(f.context + t),
        lambda t: r(f.prevc + t), 0, pos_role, neg_role, pool1, slots, cpool1,
    )

    def index1(p):
        slot = r(f.lastspot + p)
        return jnp.where(slot < 0, p, slots + slot)

    pack(pool1, ((near1, slots),), index1)
    send_near1 = remote(near1, pool2.at[pl.ds(0, slots)], 10, swapped(*at(ro, ri + 1)))
    send_near1.start()
    pack(cpool1, ((cpool2, ctiles),), context_index(r))

    send_near1.wait()
    send_far0.wait()
    r2 = other(0, 2)
    before = other(2, 1)
    train(
        r2(f.count), lambda t: before(f.place + r2(f.vert + t)), lambda t: r2(f.prev + t),
        lambda t: r2(f.context + t), lambda t: r2(f.prevc + t), 1, pos_role, neg_role, pool2, tiles, cpool2,
    )
    following = other(3, 3)

    def index2(p):
        tile = following(f.order + p)
        slot = r2(f.last + tile)
        return jnp.where(slot < 0, before(f.place + tile), tiles + slot)

    pack(pool2, ((near2, slots),), index2)
    send_near2 = remote(near2, pool3.at[pl.ds(0, slots)], 11, at(ro, ri + 1))
    send_near2.start()
    pack(cpool2, ((csend2, ctiles),), context_index(r2))
    send_c2 = remote(csend2, cpool3.at[pl.ds(0, ctiles)], 12, (ro, ri))
    keep_c2 = pltpu.make_async_copy(csend2, cpool3.at[pl.ds(0, ctiles)], local.at[11])

    @pl.when(stays)
    def _():
        keep_c2.start()

    @pl.when(jnp.logical_not(stays))
    def _():
        send_c2.start()

    pack(pool2, ((far2, tiles - slots),), lambda p: index2(slots + p))
    send_far2 = remote(far2, last.at[pl.ds(slots, tiles - slots)], 13, at(ro + 1, ri + 1))
    send_far2.start()

    for copy in here[4:]:
        copy.wait()
    send_near2.wait()

    @pl.when(stays)
    def _():
        keep_c2.wait()

    @pl.when(jnp.logical_not(stays))
    def _():
        send_c2.wait()

    m3 = mine(3)
    train(
        m3(f.count), lambda t: m3(f.spot + t), lambda t: m3(f.prev + t), lambda t: m3(f.context + t),
        lambda t: m3(f.prevc + t), 1, pos_home, neg_home, pool3, slots, cpool3,
    )

    def index3(p):
        slot = m3(f.lastspot + p)
        return jnp.where(slot < 0, p, slots + slot)

    pack(pool3, ((near3, slots),), index3)
    send_near3 = remote(near3, last.at[pl.ds(0, slots)], 14, at(o + 1, i))
    send_near3.start()
    pack(cpool3, ((csend0, ctiles),), context_index(m3))
    put_c = pltpu.make_async_copy(csend0, c_out, local.at[12])
    put_c.start()
    send_far2.wait()
    send_near3.wait()
    final = other(4, 3)
    pack(last, ((out, tiles),), lambda k: final(f.place + k))
    put_v = pltpu.make_async_copy(out, v_out, local.at[13])
    put_v.start()
    put_c.wait()
    put_v.wait()


ANY = pl.BlockSpec(memory_space=pl.ANY)
SMEM = pl.BlockSpec(memory_space=pltpu.SMEM)
VMEM = pl.BlockSpec(memory_space=pltpu.VMEM)


def body(vertex, context, tile_count, tile_vert, tile_context, positives, negatives):
    steps, slots = tile_vert.shape
    width = vertex.shape[1]
    tiles, ctiles = vertex.shape[0] // TILE, context.shape[0] // TILE
    f32, i32 = jnp.float32, jnp.int32
    meta = tables(tile_count, tile_vert, tile_context, tiles, ctiles)
    v = vertex.reshape(tiles, TILE, width)
    c = context.reshape(ctiles, TILE, width)

    def block(n):
        return pltpu.VMEM((n, TILE, width), f32)

    far = tiles - slots
    scratch = [
        block(tiles + slots), block(2 * slots), block(tiles + slots), block(2 * slots),
        *[block(ctiles + slots)] * 4,
        block(slots), block(far), block(slots), block(slots), block(far), block(slots),
        block(ctiles), block(ctiles), block(tiles), block(tiles),
        pltpu.VMEM((5,) + meta.shape, i32), pltpu.SMEM((5,) + meta.shape, i32),
        *[pltpu.VMEM((2,) + positives.shape[1:], i32), pltpu.VMEM((2,) + negatives.shape[1:], i32)] * 2,
        pltpu.SemaphoreType.DMA((15,)), pltpu.SemaphoreType.DMA((15,)), pltpu.SemaphoreType.DMA((14,)),
    ]
    v, c = pl.pallas_call(
        functools.partial(kernel, (tiles, slots, ctiles)),
        out_shape=(jax.ShapeDtypeStruct(v.shape, f32), jax.ShapeDtypeStruct(c.shape, f32)),
        in_specs=[VMEM, SMEM] + [ANY] * 4,
        out_specs=(ANY, ANY),
        scratch_shapes=scratch,
        compiler_params=pltpu.CompilerParams(has_side_effects=True, vmem_limit_bytes=60 * 1024 * 1024),
    )(meta, meta, v, c, positives, negatives)
    return v.reshape(vertex.shape), c.reshape(context.shape)


def solution(mesh):
    lists = P(("outer", "inner"))
    rows = P(("outer", "inner"), None)
    return jax.shard_map(
        body,
        mesh=mesh,
        in_specs=(
            rows, rows, lists, rows, rows,
            P(("outer", "inner"), None, None), P(("outer", "inner"), None, None, None),
        ),
        out_specs=(rows, rows),
        check_vma=False,
    )
```

profile of v0, /device:TPU:0, one launch (start us, length us, event | category | flops | bytes accessed | tf_op | source)
XLA Modules:
  0.0 144.6 jit_solution(12468000697544123332)
XLA Ops:
  0.6 0.8 fusion
  1.4 0.1 convert_reduce_fusion
  1.5 0.7 copy.10
  2.3 0.1 select_reduce_fusion.1
  2.4 0.1 subtract_select_fusion
  2.5 0.2 select_reduce_fusion
  2.7 0.9 select_reduce_fusion.6
  3.6 1.1 select_reduce_fusion.2
  4.7 0.8 concatenate.3
  5.5 0.6 pad.4.meta.meta_s
  6.1 134.4 %shard_map.86 = (f32[16,256,128]{2,1,0:T(8,128)}, f32[8,256,128]{2,1,0:T(8,128)}) custom-call(s32[8,128]{1,0:T(8,128)} %pad.4.meta.meta_s, s32[8,128]{1,0:T(8,128)} %pad.4.meta.meta_s, f32[16,256,128]{2,1,0:T(8,128)} %bitcast.5, f32[8,256,128]{2,1,0:T(8,128)} %bitcast.7, s32[4,8,256]{2,1,0:T(8,128)} %positives.1, s32[4,8,4,256]{3,2,1,0:T(4,128)} %negatives.1), custom_call_target="tpu_custom_call" | custom-call | tf_op jit(solution)/shard_map/pallas_call | solution.py:364
  140.5 0.0 copy-start
  140.5 3.1 %copy.13 = f32[4096,128]{1,0:T(8,128)} copy(f32[4096,128]{1,0:T(8,128)} %bitcast.6) | data formatting | bytes 4194304
  143.6 0.0 copy-done
  143.6 1.0 copy.14
  (3 shorter events, 0.0 us)
Async XLA Ops:
  140.5 3.1 %copy-start = (f32[8,256,128]{2,1,0:T(8,128)S(1)}, f32[8,256,128]{2,1,0:T(8,128)}, u32[]{:S(2)}) copy-start(f32[8,256,128]{2,1,0:T(8,128)} %get-tuple-element.5) | copy-start | bytes 3145732
where the time goes:
time: 145 us
  Pallas kernels  134 us (92%)
  local copies, waits for them, and re-layouts  6.25 us (4%)
  other arithmetic  3.32 us (2%)
    pallas_call x1, Pallas kernels, body(): pl.pallas_call(functools.partial(kernel, (tiles, slots, ctiles)), out_sha...  134 us
    unnamed x4, local copies, waits for them, and re-layouts  4.11 us

commit v1 on v0

--- a/solution.py
+++ b/solution.py
@@ -37,37 +37,60 @@
         self.width = -(-start // 128) * 128
 
 
-def tables(tile_count, tile_vert, tile_context, tiles, ctiles):
-    steps, slots = tile_vert.shape
-    i32 = jnp.int32
-    ks = jnp.arange(tiles, dtype=i32)
-    cs = jnp.arange(ctiles, dtype=i32)
-    ts = jnp.arange(slots, dtype=i32)
-    is_tile = tile_vert[:, :, None] == ks
-    marked = jnp.any(is_tile, 1).astype(i32)
-    before = jnp.sum(jnp.where(ks[None, :, None] > ks[None, None, :], marked[:, None, :], 0), -1)
-    total = jnp.sum(marked, -1, keepdims=True)
-    place = jnp.where(marked == 1, before, total + ks - before)
-    order = jnp.sum(jnp.where(place[:, None, :] == ks[None, :, None], ks, 0), -1)
-    last = jnp.max(jnp.where(is_tile, ts[None, :, None], -1), 1)
-    spot = jnp.sum(jnp.where(is_tile, place[:, None, :], 0), -1)
-    earlier = ts[None, :, None] > ts[None, None, :]
-    prev = jnp.max(jnp.where(earlier & (tile_vert[:, :, None] == tile_vert[:, None, :]), ts, -1), -1)
-    lastspot = jnp.max(jnp.where(spot[:, None, :] == ts[None, :, None], ts, -1), -1)
-    prevc = jnp.max(jnp.where(earlier & (tile_context[:, :, None] == tile_context[:, None, :]), ts, -1), -1)
-    lastc = jnp.max(jnp.where(tile_context[:, None, :] == cs[None, :, None], ts, -1), -1)
-    rows = jnp.concatenate(
-        [place, order, last, spot, prev, lastspot, tile_vert, tile_context, prevc, lastc, tile_count[:, None]], 1
-    )
-    width = Fields(tiles, slots, ctiles).width
-    return jnp.pad(rows, ((0, -steps % 8), (0, width - rows.shape[1])))
+def tables(f, tiles, slots, ctiles, count, vert, context):
+    steps = vert.shape[0]
+    shape = (steps, f.width)
+    col = lax.broadcasted_iota(jnp.int32, shape, 1)
+    row = lax.broadcasted_iota(jnp.int32, shape, 0)
+    v = [jnp.broadcast_to(vert[:, t : t + 1], shape) for t in range(slots)]
+    c = [jnp.broadcast_to(context[:, t : t + 1], shape) for t in range(slots)]
+
+    def latest(values, at, upto=slots):
+        found = jnp.full(shape, -1, jnp.int32)
+        for t in range(upto):
+            found = jnp.where(values[t] == at, t, found)
+        return found
+
+    first = [jnp.where(latest(v, v[t], t) < 0, 1, 0) for t in range(slots)]
+    total = functools.reduce(lambda x, y: x + y, first)
+
+    def before(at):
+        return functools.reduce(lambda x, y: x + y, [jnp.where(v[t] < at, first[t], 0) for t in range(slots)])
+
+    def place(at):
+        count_before = before(at)
+        return jnp.where(latest(v, at) >= 0, count_before, total + at - count_before)
+
+    order = jnp.zeros(shape, jnp.int32)
+    for k in range(tiles):
+        order = jnp.where(place(jnp.full(shape, k, jnp.int32)) == col - f.order, k, order)
+    out = jnp.zeros(shape, jnp.int32)
+
+    def put(start, size, value):
+        return jnp.where((col >= start) & (col < start + size), value, out)
+
+    out = put(f.place, tiles, place(col - f.place))
+    out = put(f.order, tiles, order)
+    out = put(f.last, tiles, latest(v, col - f.last))
+    spots = [before(v[t]) for t in range(slots)]
+    out = put(f.lastspot, slots, latest(spots, col - f.lastspot))
+    out = put(f.lastc, ctiles, latest(c, col - f.lastc))
+    for t in range(slots):
+        out = put(f.spot + t, 1, spots[t])
+        out = put(f.prev + t, 1, latest(v, v[t], t))
+        out = put(f.prevc + t, 1, latest(c, c[t], t))
+        out = put(f.vert + t, 1, v[t])
+        out = put(f.context + t, 1, c[t])
+    for s in range(steps):
+        out = jnp.where((row == s) & (col == f.count), count[s], out)
+    return out
 
 
 def kernel(
-    sizes, meta, meta_s, vertex, context, positives, negatives, v_out, c_out,
+    sizes, tile_count, tile_vert, tile_context, vertex, context, positives, negatives, v_out, c_out,
     pool0, pool1, pool2, pool3, cpool0, cpool1, cpool2, cpool3,
     near0, far0, near1, near2, far2, near3, csend0, csend2, last, out,
-    lists_v, lists, pos_home, neg_home, pos_role, neg_role, send, recv, local,
+    relay_a, relay_b, relay_c, vert_v, context_v, meta, meta_s, lists_v, lists, pos_home, neg_home, pos_role, neg_role, send, recv, local,
 ):
     tiles, slots, ctiles = sizes
     f = Fields(tiles, slots, ctiles)
@@ -83,11 +106,24 @@
     ro, ri = swapped(o, i)
     stays = o % 2 == i % 2
 
-    def remote(source, target, k, device):
+    pair = (o % 2, i % 2)
+
+    def when(*kinds):
+        ok = [(pair[0] == a) & (pair[1] == b) for a, b in kinds]
+        return pl.when(functools.reduce(jnp.logical_or, ok))
+
+    def remote(source, target, k, device, into=None):
         return pltpu.make_async_remote_copy(
-            src_ref=source, dst_ref=target, send_sem=send.at[k], recv_sem=recv.at[k],
+            src_ref=source, dst_ref=target, send_sem=send.at[k], recv_sem=recv.at[k if into is None else into],
             device_id=device, device_id_type=MESH,
         )
+
+    load = [
+        pltpu.make_async_copy(tile_vert, vert_v, local.at[14]),
+        pltpu.make_async_copy(tile_context, context_v, local.at[15]),
+    ]
+    for copy in load:
+        copy.start()
 
     here = [
         pltpu.make_async_copy(vertex, pool0.at[pl.ds(0, tiles)], local.at[0]),
@@ -99,6 +135,33 @@
     ]
     for copy in here:
         copy.start()
+
+    barrier = pltpu.get_barrier_semaphore()
+    sources = [
+        at(o, i + 1), (ro, ri - 1), (ro, ri + 1), at(o - 1, i), swapped(*at(ro, ri - 1)),
+        swapped(*at(o, i - 1)), swapped(*at(o - 1, i - 1)), at(o, i - 2), at(o - 2, i),
+    ]
+    for source in sources:
+        pl.semaphore_signal(barrier, inc=1, device_id=at(*source), device_id_type=MESH)
+
+    @pl.when(jnp.logical_not(stays))
+    def _():
+        pl.semaphore_signal(barrier, inc=1, device_id=(ro, ri), device_id_type=MESH)
+
+    for copy in load:
+        copy.wait()
+    meta[...] = jnp.zeros_like(meta)
+    meta[pl.ds(0, vert_v.shape[0])] = tables(f, tiles, slots, ctiles, tile_count, vert_v, context_v)
+    own_meta = pltpu.make_async_copy(meta, meta_s, local.at[16])
+    own_meta.start()
+
+    @pl.when(stays)
+    def _():
+        pl.semaphore_wait(barrier, len(sources))
+
+    @pl.when(jnp.logical_not(stays))
+    def _():
+        pl.semaphore_wait(barrier, len(sources) + 1)
 
     sends = [
         remote(meta, lists_v.at[1], 1, at(o, i - 1)),
@@ -187,6 +250,7 @@
     def other(which, s):
         return lambda k: lists[which, s, k]
 
+    own_meta.wait()
     for copy in here[:4]:
         copy.wait()
     m = mine(0)
@@ -234,8 +298,24 @@
         send_c0.start()
 
     pack(pool0, ((far0, tiles - slots),), lambda p: index0(slots + p))
-    send_far0 = remote(far0, pool2.at[pl.ds(slots, tiles - slots)], 9, swapped(*at(o, i + 2)))
-    send_far0.start()
+    rest2 = pool2.at[pl.ds(slots, tiles - slots)]
+    send_far0 = remote(far0, rest2, 9, at(o, i + 2))
+    far0_a = remote(far0, relay_a, 15, at(o, i + 2))
+    far0_b = remote(far0, relay_b, 16, (ro, ri))
+    pass_a = remote(relay_a, rest2, 17, (ro, ri), 9)
+    pass_b = remote(relay_b, rest2, 18, at(o, i + 2), 9)
+
+    @when((0, 0))
+    def _():
+        send_far0.start()
+
+    @when((1, 0))
+    def _():
+        far0_a.start()
+
+    @when((0, 1))
+    def _():
+        far0_b.start()
 
     send_near0.wait()
 
@@ -260,10 +340,22 @@
     pack(pool1, ((near1, slots),), index1)
     send_near1 = remote(near1, pool2.at[pl.ds(0, slots)], 10, swapped(*at(ro, ri + 1)))
     send_near1.start()
+
+    @when((1, 1))
+    def _():
+        send_far0.start()
+
+    @when((1, 0))
+    def _():
+        far0_a.wait_recv()
+        pass_a.start()
+        far0_b.wait_recv()
+        pass_b.start()
+
     pack(cpool1, ((cpool2, ctiles),), context_index(r))
 
     send_near1.wait()
-    send_far0.wait()
+    send_far0.wait_recv()
     r2 = other(0, 2)
     before = other(2, 1)
     train(
@@ -293,8 +385,18 @@
         send_c2.start()
 
     pack(pool2, ((far2, tiles - slots),), lambda p: index2(slots + p))
-    send_far2 = remote(far2, last.at[pl.ds(slots, tiles - slots)], 13, at(ro + 1, ri + 1))
-    send_far2.start()
+    rest3 = last.at[pl.ds(slots, tiles - slots)]
+    send_far2 = remote(far2, rest3, 13, at(ro + 1, ri + 1))
+    far2_c = remote(far2, relay_c, 19, at(o + 2, i))
+    pass_c = remote(relay_c, rest3, 20, at(o - 1, i + 1), 13)
+
+    @when((1, 1))
+    def _():
+        far2_c.start()
+
+    @when((0, 0), (0, 1), (1, 0))
+    def _():
+        send_far2.start()
 
     for copy in here[4:]:
         copy.wait()
@@ -324,8 +426,38 @@
     pack(cpool3, ((csend0, ctiles),), context_index(m3))
     put_c = pltpu.make_async_copy(csend0, c_out, local.at[12])
     put_c.start()
-    send_far2.wait()
+
+    @when((1, 1))
+    def _():
+        far2_c.wait_recv()
+        pass_c.start()
+
+    send_far2.wait_recv()
     send_near3.wait()
+
+    @when((0, 0), (1, 1))
+    def _():
+        send_far0.wait_send()
+
+    @when((1, 0))
+    def _():
+        far0_a.wait_send()
+        pass_a.wait_send()
+        pass_b.wait_send()
+
+    @when((0, 1))
+    def _():
+        far0_b.wait_send()
+
+    @when((0, 0), (0, 1), (1, 0))
+    def _():
+        send_far2.wait_send()
+
+    @when((1, 1))
+    def _():
+        far2_c.wait_send()
+        pass_c.wait_send()
+
     final = other(4, 3)
     pack(last, ((out, tiles),), lambda k: final(f.place + k))
     put_v = pltpu.make_async_copy(out, v_out, local.at[13])
@@ -344,7 +476,7 @@
     width = vertex.shape[1]
     tiles, ctiles = vertex.shape[0] // TILE, context.shape[0] // TILE
     f32, i32 = jnp.float32, jnp.int32
-    meta = tables(tile_count, tile_vert, tile_context, tiles, ctiles)
+    meta = (-(-steps // 8) * 8, Fields(tiles, slots, ctiles).width)
     v = vertex.reshape(tiles, TILE, width)
     c = context.reshape(ctiles, TILE, width)
 
@@ -357,18 +489,21 @@
         *[block(ctiles + slots)] * 4,
         block(slots), block(far), block(slots), block(slots), block(far), block(slots),
         block(ctiles), block(ctiles), block(tiles), block(tiles),
-        pltpu.VMEM((5,) + meta.shape, i32), pltpu.SMEM((5,) + meta.shape, i32),
+        block(far), block(far), block(far),
+        pltpu.VMEM(tile_vert.shape, i32), pltpu.VMEM(tile_context.shape, i32),
+        pltpu.VMEM(meta, i32), pltpu.SMEM(meta, i32),
+        pltpu.VMEM((5,) + meta, i32), pltpu.SMEM((5,) + meta, i32),
         *[pltpu.VMEM((2,) + positives.shape[1:], i32), pltpu.VMEM((2,) + negatives.shape[1:], i32)] * 2,
-        pltpu.SemaphoreType.DMA((15,)), pltpu.SemaphoreType.DMA((15,)), pltpu.SemaphoreType.DMA((14,)),
+        pltpu.SemaphoreType.DMA((21,)), pltpu.SemaphoreType.DMA((21,)), pltpu.SemaphoreType.DMA((17,)),
     ]
     v, c = pl.pallas_call(
         functools.partial(kernel, (tiles, slots, ctiles)),
         out_shape=(jax.ShapeDtypeStruct(v.shape, f32), jax.ShapeDtypeStruct(c.shape, f32)),
-        in_specs=[VMEM, SMEM] + [ANY] * 4,
+        in_specs=[SMEM] + [ANY] * 6,
         out_specs=(ANY, ANY),
         scratch_shapes=scratch,
-        compiler_params=pltpu.CompilerParams(has_side_effects=True, vmem_limit_bytes=60 * 1024 * 1024),
-    )(meta, meta, v, c, positives, negatives)
+        compiler_params=pltpu.CompilerParams(collective_id=0, has_side_effects=True, vmem_limit_bytes=50 * 1024 * 1024),
+    )(tile_count, tile_vert, tile_context, v, c, positives, negatives)
     return v.reshape(vertex.shape), c.reshape(context.shape)
 
 

time: 145 us -> 122 us (0.84)
  Pallas kernels: 134 us -> 112 us
  other arithmetic: 3.32 us -> 0 us
  local copies, waits for them, and re-layouts: 6.25 us -> 8.91 us
    pallas_call x1, Pallas kernels: 134 us -> 112 us  [body(): pl.pallas_call(functools.partial(kernel, (tiles, slots, ctiles)), out_sha...]
    unnamed x4 -> x14, local copies, waits for them, and re-layouts: 4.11 us -> 8.91 us
where the time goes in v1:
time: 122 us
  Pallas kernels  112 us (92%)
  local copies, waits for them, and re-layouts  8.91 us (7%)
    pallas_call x1, Pallas kernels, body(): pl.pallas_call(functools.partial(kernel, (tiles, slots, ctiles)), out_sha...  112 us
    unnamed x14, local copies, waits for them, and re-layouts  8.91 us

profile of v1, /device:TPU:0, one launch (start us, length us, event | category | flops | bytes accessed | tf_op | source)
XLA Modules:
  0.0 121.9 jit_solution(6210649012257107712)
XLA Ops:
  0.6 0.0 copy-start
  0.6 1.2 copy-done
  1.9 0.0 copy-start.1
  1.9 0.9 copy-done.1
  2.8 0.0 copy-start.2
  2.8 0.8 copy-done.2
  3.5 0.0 copy-start.3
  3.5 0.7 copy-done.3
  4.2 0.0 copy-start.4
  4.2 0.7 copy-done.4
  4.9 0.0 copy-start.5
  4.9 0.7 copy-done.5
  5.5 112.3 %shard_map.86 = (f32[16,256,128]{2,1,0:T(8,128)}, f32[8,256,128]{2,1,0:T(8,128)S(1)}) custom-call(s32[4]{0:T(128)S(1)} %copy-done.5, s32[4,8]{1,0:T(4,128)S(1)} %copy-done.3, s32[4,8]{1,0:T(4,128)S(1)} %copy-done.4, f32[16,256,128]{2,1,0:T(8,128)} %bitcast.6, f32[8,256,128]{2,1,0:T(8,128)S(1)} %bitcast.5, s32[4,8,256]{2,1,0:T(8,128)S(1)} %copy-done.2, ...), custom_call_target="tpu_custom_call" | custom-call | tf_op jit(solution)/shard_map/pallas_call | solution.py:499
  117.9 3.0 %copy.11 = f32[4096,128]{1,0:T(8,128)} copy(f32[4096,128]{1,0:T(8,128)} %bitcast.7) | data formatting | bytes 4194304
  120.9 1.0 copy.12
Async XLA Ops:
  0.6 1.2 %copy-start = (f32[2048,128]{1,0:T(8,128)S(1)}, f32[2048,128]{1,0:T(8,128)}, u32[]{:S(2)}) copy-start(f32[2048,128]{1,0:T(8,128)} %param.8) | copy-start | bytes 3145732
  1.9 0.9 copy-start.1
  2.8 0.8 copy-start.2
  3.5 0.7 copy-start.3
  4.2 0.7 copy-start.4
  4.9 0.7 copy-start.5

commit v2 on v1

--- a/solution.py
+++ b/solution.py
@@ -89,8 +89,8 @@
 def kernel(
     sizes, tile_count, tile_vert, tile_context, vertex, context, positives, negatives, v_out, c_out,
     pool0, pool1, pool2, pool3, cpool0, cpool1, cpool2, cpool3,
-    near0, far0, near1, near2, far2, near3, csend0, csend2, last, out,
-    relay_a, relay_b, relay_c, vert_v, context_v, meta, meta_s, lists_v, lists, pos_home, neg_home, pos_role, neg_role, send, recv, local,
+    idle0, busy0, relay_idle, relay_busy, near1, rest1, rest, near2, far2, relay_c, near3, csend0, csend2, last, out,
+    vert_v, context_v, meta, meta_s, lists_v, lists, pos_home, neg_home, pos_role, neg_role, send, recv, local,
 ):
     tiles, slots, ctiles = sizes
     f = Fields(tiles, slots, ctiles)
@@ -139,7 +139,7 @@
     barrier = pltpu.get_barrier_semaphore()
     sources = [
         at(o, i + 1), (ro, ri - 1), (ro, ri + 1), at(o - 1, i), swapped(*at(ro, ri - 1)),
-        swapped(*at(o, i - 1)), swapped(*at(o - 1, i - 1)), at(o, i - 2), at(o - 2, i),
+        swapped(*at(o, i - 1)), swapped(*at(o - 1, i - 1)), at(o - 2, i),
     ]
     for source in sources:
         pl.semaphore_signal(barrier, inc=1, device_id=at(*source), device_id_type=MESH)
@@ -164,10 +164,9 @@
         pl.semaphore_wait(barrier, len(sources) + 1)
 
     sends = [
-        remote(meta, lists_v.at[1], 1, at(o, i - 1)),
-        remote(meta, lists_v.at[2], 2, swapped(*at(o, i + 1))),
-        remote(meta, lists_v.at[3], 3, swapped(*at(o, i - 1))),
-        remote(meta, lists_v.at[4], 4, at(o + 1, i)),
+        remote(meta, lists_v.at[1], 1, swapped(*at(o, i + 1))),
+        remote(meta, lists_v.at[2], 2, swapped(*at(o, i - 1))),
+        remote(meta, lists_v.at[3], 3, at(o + 1, i)),
     ]
     for copy in sends:
         copy.start()
@@ -250,41 +249,64 @@
     def other(which, s):
         return lambda k: lists[which, s, k]
 
+    def parts(n, most):
+        count = most if n % most == 0 else 1
+        return [(k * (n // count), n // count) for k in range(count)]
+
+    far = tiles - slots
+    idle_parts, busy_parts = parts(far, 2), parts(slots, 4)
+
+    def moves(source, relay, start, pieces, k):
+        direct, up, on = [], [], []
+        for j, (begin, size) in enumerate(pieces):
+            piece = pl.ds(begin, size)
+            target = pool1.at[pl.ds(start + begin, size)]
+            direct.append(remote(source.at[piece], target, k + j, swapped(*at(o, i + 1))))
+            up.append(remote(source.at[piece], relay.at[piece], k + 6 + j, at(o, i - 1)))
+            on.append(remote(relay.at[piece], target, k + 12 + j, at(o, i + 2), k + j))
+        return direct, up, on
+
+    idle_direct, idle_up, idle_on = moves(idle0, relay_idle, slots, idle_parts, 20)
+    busy_direct, busy_up, busy_on = moves(busy0, relay_busy, 0, busy_parts, 22)
+    straight = when((0, 0), (1, 0), (1, 1))
+
+    def begin(copies):
+        for copy in copies:
+            copy.start()
+
     own_meta.wait()
-    for copy in here[:4]:
+    m = mine(0)
+    here[0].wait()
+    pack(pool0, ((idle0, far),), lambda p: m(f.order + slots + p))
+
+    @straight
+    def _():
+        begin(idle_direct)
+
+    @when((0, 1))
+    def _():
+        begin(idle_up)
+
+    for copy in here[1:4]:
         copy.wait()
-    m = mine(0)
     train(
         m(f.count), lambda t: m(f.vert + t), lambda t: m(f.prev + t), lambda t: m(f.context + t),
         lambda t: m(f.prevc + t), 0, pos_home, neg_home, pool0, tiles, cpool0,
     )
-    for copy in sends:
-        copy.wait()
-
-    @pl.when(stays)
-    def _():
-        for copy in own_copies:
-            copy.wait()
-
-    @pl.when(jnp.logical_not(stays))
-    def _():
-        for copy in role_copies:
-            copy.wait()
-
-    to_smem = pltpu.make_async_copy(lists_v, lists, local.at[9])
-    to_smem.start()
-    to_smem.wait()
-
-    after = other(1, 1)
 
     def index0(p):
-        tile = after(f.order + p)
+        tile = m(f.order + p)
         slot = m(f.last + tile)
         return jnp.where(slot < 0, tile, tiles + slot)
 
-    pack(pool0, ((near0, slots),), index0)
-    send_near0 = remote(near0, pool1.at[pl.ds(0, slots)], 7, swapped(*at(o, i + 1)))
-    send_near0.start()
+    for j, (start, size) in enumerate(busy_parts):
+        for p in range(start, start + size):
+            busy0[p] = pool0[index0(p)]
+
+        @straight
+        def _():
+            busy_direct[j].start()
+
     pack(cpool0, ((csend0, ctiles),), context_index(m))
     send_c0 = remote(csend0, cpool1.at[pl.ds(0, ctiles)], 8, (ro, ri))
     keep_c0 = pltpu.make_async_copy(csend0, cpool1.at[pl.ds(0, ctiles)], local.at[10])
@@ -297,27 +319,36 @@
     def _():
         send_c0.start()
 
-    pack(pool0, ((far0, tiles - slots),), lambda p: index0(slots + p))
-    rest2 = pool2.at[pl.ds(slots, tiles - slots)]
-    send_far0 = remote(far0, rest2, 9, at(o, i + 2))
-    far0_a = remote(far0, relay_a, 15, at(o, i + 2))
-    far0_b = remote(far0, relay_b, 16, (ro, ri))
-    pass_a = remote(relay_a, rest2, 17, (ro, ri), 9)
-    pass_b = remote(relay_b, rest2, 18, at(o, i + 2), 9)
+    @when((0, 1))
+    def _():
+        begin(busy_up)
+
+    for copy in sends:
+        copy.wait()
+
+    @pl.when(stays)
+    def _():
+        for copy in own_copies:
+            copy.wait()
+
+    @pl.when(jnp.logical_not(stays))
+    def _():
+        for copy in role_copies:
+            copy.wait()
+
+    to_smem = pltpu.make_async_copy(lists_v, lists, local.at[9])
+    to_smem.start()
 
     @when((0, 0))
     def _():
-        send_far0.start()
-
-    @when((1, 0))
-    def _():
-        far0_a.start()
-
-    @when((0, 1))
-    def _():
-        far0_b.start()
-
-    send_near0.wait()
+        for arrived, passed in zip(idle_up + busy_up, idle_on + busy_on):
+            arrived.wait_recv()
+            passed.start()
+
+    to_smem.wait()
+
+    for copy in idle_direct + busy_direct:
+        copy.wait_recv()
 
     @pl.when(stays)
     def _():
@@ -328,47 +359,42 @@
         send_c0.wait()
 
     r = other(0, 1)
+    before = other(1, 0)
     train(
-        r(f.count), lambda t: r(f.spot + t), lambda t: r(f.prev + t), lambda t: r(f.context + t),
-        lambda t: r(f.prevc + t), 0, pos_role, neg_role, pool1, slots, cpool1,
+        r(f.count), lambda t: before(f.place + r(f.vert + t)), lambda t: r(f.prev + t),
+        lambda t: r(f.context + t), lambda t: r(f.prevc + t), 0, pos_role, neg_role, pool1, tiles, cpool1,
     )
+    second = other(2, 2)
 
     def index1(p):
-        slot = r(f.lastspot + p)
-        return jnp.where(slot < 0, p, slots + slot)
+        tile = second(f.order + p)
+        slot = r(f.last + tile)
+        return jnp.where(slot < 0, before(f.place + tile), tiles + slot)
 
     pack(pool1, ((near1, slots),), index1)
     send_near1 = remote(near1, pool2.at[pl.ds(0, slots)], 10, swapped(*at(ro, ri + 1)))
     send_near1.start()
-
-    @when((1, 1))
-    def _():
-        send_far0.start()
-
-    @when((1, 0))
-    def _():
-        far0_a.wait_recv()
-        pass_a.start()
-        far0_b.wait_recv()
-        pass_b.start()
-
+    pack(pool1, ((rest1, far),), lambda p: index1(slots + p))
+    send_rest1 = remote(rest1, rest, 9, swapped(*at(ro, ri + 1)))
+    send_rest1.start()
     pack(cpool1, ((cpool2, ctiles),), context_index(r))
 
     send_near1.wait()
-    send_far0.wait_recv()
     r2 = other(0, 2)
-    before = other(2, 1)
     train(
-        r2(f.count), lambda t: before(f.place + r2(f.vert + t)), lambda t: r2(f.prev + t),
+        r2(f.count), lambda t: r2(f.spot + t), lambda t: r2(f.prev + t),
         lambda t: r2(f.context + t), lambda t: r2(f.prevc + t), 1, pos_role, neg_role, pool2, tiles, cpool2,
     )
-    following = other(3, 3)
+    following = other(2, 3)
 
     def index2(p):
         tile = following(f.order + p)
         slot = r2(f.last + tile)
-        return jnp.where(slot < 0, before(f.place + tile), tiles + slot)
-
+        return jnp.where(slot < 0, r2(f.place + tile), tiles + slot)
+
+    send_rest1.wait()
+    for k in range(far):
+        pool2[slots + k] = rest[k]
     pack(pool2, ((near2, slots),), index2)
     send_near2 = remote(near2, pool3.at[pl.ds(0, slots)], 11, at(ro, ri + 1))
     send_near2.start()
@@ -384,11 +410,11 @@
     def _():
         send_c2.start()
 
-    pack(pool2, ((far2, tiles - slots),), lambda p: index2(slots + p))
+    pack(pool2, ((far2, far),), lambda p: index2(slots + p))
     rest3 = last.at[pl.ds(slots, tiles - slots)]
     send_far2 = remote(far2, rest3, 13, at(ro + 1, ri + 1))
-    far2_c = remote(far2, relay_c, 19, at(o + 2, i))
-    pass_c = remote(relay_c, rest3, 20, at(o - 1, i + 1), 13)
+    far2_c = remote(far2, relay_c, 14, at(o + 2, i))
+    pass_c = remote(relay_c, rest3, 15, at(o - 1, i + 1), 13)
 
     @when((1, 1))
     def _():
@@ -421,7 +447,7 @@
         return jnp.where(slot < 0, p, slots + slot)
 
     pack(pool3, ((near3, slots),), index3)
-    send_near3 = remote(near3, last.at[pl.ds(0, slots)], 14, at(o + 1, i))
+    send_near3 = remote(near3, last.at[pl.ds(0, slots)], 16, at(o + 1, i))
     send_near3.start()
     pack(cpool3, ((csend0, ctiles),), context_index(m3))
     put_c = pltpu.make_async_copy(csend0, c_out, local.at[12])
@@ -435,19 +461,20 @@
     send_far2.wait_recv()
     send_near3.wait()
 
-    @when((0, 0), (1, 1))
-    def _():
-        send_far0.wait_send()
-
-    @when((1, 0))
-    def _():
-        far0_a.wait_send()
-        pass_a.wait_send()
-        pass_b.wait_send()
+    @straight
+    def _():
+        for copy in idle_direct + busy_direct:
+            copy.wait_send()
 
     @when((0, 1))
     def _():
-        far0_b.wait_send()
+        for copy in idle_up + busy_up:
+            copy.wait_send()
+
+    @when((0, 0))
+    def _():
+        for copy in idle_on + busy_on:
+            copy.wait_send()
 
     @when((0, 0), (0, 1), (1, 0))
     def _():
@@ -458,7 +485,7 @@
         far2_c.wait_send()
         pass_c.wait_send()
 
-    final = other(4, 3)
+    final = other(3, 3)
     pack(last, ((out, tiles),), lambda k: final(f.place + k))
     put_v = pltpu.make_async_copy(out, v_out, local.at[13])
     put_v.start()
@@ -466,7 +493,7 @@
     put_v.wait()
 
 
-ANY = pl.BlockSpec(memory_space=pl.ANY)
+HBM = pl.BlockSpec(memory_space=pltpu.HBM)
 SMEM = pl.BlockSpec(memory_space=pltpu.SMEM)
 VMEM = pl.BlockSpec(memory_space=pltpu.VMEM)
 
@@ -485,24 +512,24 @@
 
     far = tiles - slots
     scratch = [
-        block(tiles + slots), block(2 * slots), block(tiles + slots), block(2 * slots),
+        block(tiles + slots), block(tiles + slots), block(tiles + slots), block(2 * slots),
         *[block(ctiles + slots)] * 4,
-        block(slots), block(far), block(slots), block(slots), block(far), block(slots),
+        block(far), block(slots), block(far), block(slots), block(slots), block(far), block(far),
+        block(slots), block(far), block(far), block(slots),
         block(ctiles), block(ctiles), block(tiles), block(tiles),
-        block(far), block(far), block(far),
         pltpu.VMEM(tile_vert.shape, i32), pltpu.VMEM(tile_context.shape, i32),
         pltpu.VMEM(meta, i32), pltpu.SMEM(meta, i32),
-        pltpu.VMEM((5,) + meta, i32), pltpu.SMEM((5,) + meta, i32),
+        pltpu.VMEM((4,) + meta, i32), pltpu.SMEM((4,) + meta, i32),
         *[pltpu.VMEM((2,) + positives.shape[1:], i32), pltpu.VMEM((2,) + negatives.shape[1:], i32)] * 2,
-        pltpu.SemaphoreType.DMA((21,)), pltpu.SemaphoreType.DMA((21,)), pltpu.SemaphoreType.DMA((17,)),
+        pltpu.SemaphoreType.DMA((40,)), pltpu.SemaphoreType.DMA((40,)), pltpu.SemaphoreType.DMA((17,)),
     ]
     v, c = pl.pallas_call(
         functools.partial(kernel, (tiles, slots, ctiles)),
         out_shape=(jax.ShapeDtypeStruct(v.shape, f32), jax.ShapeDtypeStruct(c.shape, f32)),
-        in_specs=[SMEM] + [ANY] * 6,
-        out_specs=(ANY, ANY),
+        in_specs=[SMEM] + [HBM] * 6,
+        out_specs=(HBM, HBM),
         scratch_shapes=scratch,
-        compiler_params=pltpu.CompilerParams(collective_id=0, has_side_effects=True, vmem_limit_bytes=50 * 1024 * 1024),
+        compiler_params=pltpu.CompilerParams(collective_id=0, has_side_effects=True, vmem_limit_bytes=67_043_328),
     )(tile_count, tile_vert, tile_context, v, c, positives, negatives)
     return v.reshape(vertex.shape), c.reshape(context.shape)
 

time: 122 us -> 118 us (0.967)
  the two profiles are of different devices: /device:TPU:0 before, /device:TPU:8 now
where the time goes in v2:
time: 118 us; the launch traced here: 117 us
  Pallas kernels  113 us (96%)
  local copies, waits for them, and re-layouts  4.11 us (3%)
    pallas_call x1, Pallas kernels, body(): pl.pallas_call(functools.partial(kernel, (tiles, slots, ctiles)), out_sha...  113 us
    unnamed x4, local copies, waits for them, and re-layouts  4.11 us

profile of v2, /device:TPU:8, one launch (start us, length us, event | category | flops | bytes accessed | tf_op | source)
XLA Modules:
  0.0 117.5 jit_solution(15283653485833667151)
XLA Ops:
  0.6 112.7 %shard_map.86 = (f32[16,256,128]{2,1,0:T(8,128)}, f32[8,256,128]{2,1,0:T(8,128)}) custom-call(s32[4]{0:T(128)} %tile_count.1, s32[4,8]{1,0:T(4,128)} %tile_vert.1, s32[4,8]{1,0:T(4,128)} %tile_context.1, f32[16,256,128]{2,1,0:T(8,128)} %bitcast.4, f32[8,256,128]{2,1,0:T(8,128)} %bitcast.7, s32[4,8,256]{2,1,0:T(8,128)} %positives.1, s32[4,8,4,256]{3,2,1,0:T(4,128)} %negatives.1), custom_call_target="tpu_custom_call" | custom-call | tf_op jit(solution)/shard_map/pallas_call | solution.py:526
  113.4 0.0 copy-start
  113.4 3.1 %copy.11 = f32[4096,128]{1,0:T(8,128)} copy(f32[4096,128]{1,0:T(8,128)} %bitcast.5) | data formatting | bytes 4194304
  116.5 0.0 copy-done
  116.5 1.0 copy.12
Async XLA Ops:
  113.4 3.1 %copy-start = (f32[8,256,128]{2,1,0:T(8,128)S(1)}, f32[8,256,128]{2,1,0:T(8,128)}, u32[]{:S(2)}) copy-start(f32[8,256,128]{2,1,0:T(8,128)} %get-tuple-element.5) | copy-start | bytes 3145732
